TPU v7x, 32 devices: a whole 2x2x4 slice. The times are simulated.
32 devices in a mesh: parts: 2 (over x), outer: 8 (over z, y), inner: 2 (over core).
Axes of the slice: x: 2, y: 2, z: 4, core: 2. Of those that a mesh axis runs over, the one named last changes fastest.
Arguments:
- queries: bfloat16 [8192, 1024], P(('parts', 'outer', 'inner')), parts along dimension 0, may hold values from -72 to 72
- key_rows: bfloat16 [8192, 128], P(('parts', 'outer', 'inner')), parts along dimension 0, may hold values from -6 to 6
- value_rows: bfloat16 [8192, 128], P(('parts', 'outer', 'inner')), parts along dimension 0, may hold values from -6 to 6
- vertical: int32 [16, 8], P('parts'), parts along dimension 0, may hold values from 0 to 63, as said below
- slash_offsets: int32 [16, 8], P('parts'), parts along dimension 0, may hold values from 0 to 63, as said below
Outputs:
- attended: bfloat16 [8192, 1024], P(('parts', 'outer', 'inner')), parts along dimension 0
There are 2 independent parts, one for each index of `parts`. A program takes and returns all parts, laid end to end along the dimension named above; each array names one. Nothing has to cross between parts.
Inputs may be any that keep to these rules, and one draw needn't show every extreme that they name: `vertical`: each row holds 8 different key-block numbers, block 0 and block 63 among them. `slash_offsets`: each row holds 8 different block offsets, offset 0 and offset 64 - 1 among them.
All inputs are finite; a program needn't handle non-finite values.
Results may differ from a plain program's by a relative error of at most 0.006.
Values may be sent and summed in bfloat16 or wider, within the bound.
A program may use at most 64 MiB of HBM per device.

v0:
```python
import math

import jax
import jax.numpy as jnp
from jax import lax
from jax.sharding import PartitionSpec as P

BLK = 64


MASKED_SCORE = -1e30


def attend_block(
    running, query_heads, query_start, key_part, value_part, key_start, vertical, slash_offsets
):
    query_count = query_heads.shape[0]
    head_count = query_heads.shape[1]
    head_dim = query_heads.shape[2]
    key_count = key_part.shape[0]
    block_count = query_count // BLK
    key_tokens = key_start + jnp.arange(key_count, dtype=jnp.int32)
    key_block = key_tokens // BLK
    query_block = query_start // BLK + jnp.arange(block_count, dtype=jnp.int32)
    block_gap = query_block[:, None] - key_block[None, :]
    vertical_hit = jnp.any(vertical[:, :, None] == key_block[None, None, :], axis=1)
    slash_hit = jnp.any(slash_offsets[:, :, None, None] == block_gap[None, None], axis=1)
    live_blocks = (block_gap >= 0)[None] & (vertical_hit[:, None, :] | slash_hit)
    query_tokens = query_start + jnp.arange(query_count, dtype=jnp.int32)
    causal = (key_tokens[None, :] <= query_tokens[:, None]).reshape(block_count, BLK, key_count)
    allowed = (live_blocks[:, :, None, :] & causal[None]).reshape(
        head_count, query_count, key_count
    )

    def update(state):
        run_out, run_max, run_total = state
        scores = jnp.einsum(
            "qhd,kd->hqk", query_heads, key_part, preferred_element_type=jnp.float32
        )
        scores = scores * (1.0 / math.sqrt(head_dim))
        new_max = jnp.maximum(run_max, jnp.max(jnp.where(allowed, scores, MASKED_SCORE), axis=-1))
        weights = jnp.where(allowed, jnp.exp(scores - new_max[..., None]), 0.0)
        rescale = jnp.exp(run_max - new_max)
        new_total = run_total * rescale + jnp.sum(weights, axis=-1)
        product = jnp.einsum(
            "hqk,kd->hqd",
            weights.astype(jnp.bfloat16),
            value_part,
            preferred_element_type=jnp.float32,
        )
        new_out = run_out * rescale[..., None] + product
        return (new_out, new_max, new_total)

    def keep_same(state):
        return state

    return lax.cond(jnp.any(allowed), update, keep_same, running)


def attend_piece(running, query_heads, query_start, key_part, value_part, vertical, slash_offsets):
    length = key_part.shape[0]
    sub_rows = math.gcd(length, query_heads.shape[0])

    def one_part(part_number, state):
        offset = part_number * sub_rows
        key_slice = lax.dynamic_slice_in_dim(key_part, offset, sub_rows, 0)
        value_slice = lax.dynamic_slice_in_dim(value_part, offset, sub_rows, 0)
        return attend_block(
            state, query_heads, query_start, key_slice, value_slice, offset, vertical, slash_offsets
        )

    return lax.fori_loop(0, length // sub_rows, one_part, running)


def shards(queries, key_rows, value_rows, vertical, slash_offsets):
    query_count = queries.shape[0]
    head_count = vertical.shape[0]
    head_dim = key_rows.shape[1]
    query_heads = queries.reshape(query_count, head_count, head_dim)
    outer_place = lax.axis_index("outer")
    inner_place = lax.axis_index("inner")
    inner_count = lax.axis_size("inner")
    own_start = (outer_place * inner_count + inner_place) * query_count
    initial = (
        jnp.zeros((head_count, query_count, head_dim), jnp.float32),
        jnp.full((head_count, query_count), MASKED_SCORE, jnp.float32),
        jnp.zeros((head_count, query_count), jnp.float32),
    )
    run_out, run_max, run_total = attend_piece(
        initial,
        query_heads,
        own_start,
        lax.all_gather(key_rows, ("outer", "inner"), axis=0, tiled=True),
        lax.all_gather(value_rows, ("outer", "inner"), axis=0, tiled=True),
        vertical,
        slash_offsets,
    )
    result = run_out / run_total[..., None]
    return (
        result.transpose(1, 0, 2).reshape(query_count, head_count * head_dim).astype(jnp.bfloat16)
    )


def solution(mesh):
    in_specs = (
        P(("parts", "outer", "inner"), None),
        P(("parts", "outer", "inner"), None),
        P(("parts", "outer", "inner"), None),
        P("parts", None),
        P("parts", None),
    )
    out_specs = P(("parts", "outer", "inner"), None)
    return jax.shard_map(shards, mesh=mesh, in_specs=in_specs, out_specs=out_specs, check_vma=False)
```

profile of v0, /device:TPU:29, one launch (start us, length us, event | category | flops | bytes accessed | tf_op | source)
XLA Modules:
  0.0 214.4 jit_solution(11371558027188347198)
XLA Ops:
  8.0 1.2 copy.16
  9.6 37.2 %all-gather.3.cloned.1.call-done = bf16[4096,128]{1,0:T(8,128)(2,1)} async-done(((bf16[256,128]{1,0:T(8,128)(2,1)}), bf16[4096,128]{1,0:T(8,128)(2,1)}) %all-gather.3.cloned.1.call-update) | async-done | bytes 1048592 | tf_op jit(solution)/shard_map/all_gather | solution.py:93
  46.8 39.0 %all-gather.5.cloned.1.call-done = bf16[4096,128]{1,0:T(8,128)(2,1)} async-done(((bf16[256,128]{1,0:T(8,128)(2,1)}), bf16[4096,128]{1,0:T(8,128)(2,1)}) %all-gather.5.cloned.1.call-update) | async-done | bytes 1048592 | tf_op jit(solution)/shard_map/all_gather | solution.py:94
  85.9 120.6 %while.20 = (s32[]{:T(128)}, f32[8,256,128]{2,1,0:T(8,128)S(1)}, f32[8,256]{1,0:T(8,128)S(1)}, f32[8,256]{1,0:T(8,128)S(1)}, s32[]{:T(128)}, /*index=5*/s32[8,8]...) while((s32[]{:T(128)}, f32[8,256,128]{2,1,0:T(8,128)S(1)}, ...), condition=%wide.region_8.9_spmd, body=%wide.region_0.8_spmd.sunk | while | flops 277661440 | bytes 12782461 | solution.py:72
  86.5 1.2 and_reduce_fusion.2
  88.5 5.0 %conditional.2 = ((f32[8,256,128]{2,1,0:T(8,128)S(1)}, f32[8,256]{1,0:T(8,128)S(1)}, f32[8,256]{1,0:T(8,128)S(1)})) conditional(s32[]{:T(128)} %convert_element_type.36, (f32[8,256,128]{2,1,0:T(8,128)S(1)}, f32[8,256]{1,0:T(8,128)S(1)}, f32[8,256]{1,0:T(8,128)S(1)}) %tuple.65, (pred[8,4,64,256]{3,2,1,0:T(32,128)(4,1)S(1)}, s32[256]{0:T(256)S(1)}, ...), branch_computations={%region_4.4_spmd, %region_5.7_spmd} | conditional | flops 276369408 | bytes 12062794 | solution.py:57
  89.3 1.4 fusion
  91.4 2.0 convolution_add_fusion
  94.0 1.2 and_reduce_fusion.2
  96.0 5.0 %conditional.2 = ((f32[8,256,128]{2,1,0:T(8,128)S(1)}, f32[8,256]{1,0:T(8,128)S(1)}, f32[8,256]{1,0:T(8,128)S(1)})) conditional(s32[]{:T(128)} %convert_element_type.36, (f32[8,256,128]{2,1,0:T(8,128)S(1)}, f32[8,256]{1,0:T(8,128)S(1)}, f32[8,256]{1,0:T(8,128)S(1)}) %tuple.65, (pred[8,4,64,256]{3,2,1,0:T(32,128)(4,1)S(1)}, s32[256]{0:T(256)S(1)}, ...), branch_computations={%region_4.4_spmd, %region_5.7_spmd} | conditional | flops 276369408 | bytes 12062794 | solution.py:57
  96.9 1.4 fusion
  99.0 2.0 convolution_add_fusion
  101.6 1.2 and_reduce_fusion.2
  103.5 5.0 %conditional.2 = ((f32[8,256,128]{2,1,0:T(8,128)S(1)}, f32[8,256]{1,0:T(8,128)S(1)}, f32[8,256]{1,0:T(8,128)S(1)})) conditional(s32[]{:T(128)} %convert_element_type.36, (f32[8,256,128]{2,1,0:T(8,128)S(1)}, f32[8,256]{1,0:T(8,128)S(1)}, f32[8,256]{1,0:T(8,128)S(1)}) %tuple.65, (pred[8,4,64,256]{3,2,1,0:T(32,128)(4,1)S(1)}, s32[256]{0:T(256)S(1)}, ...), branch_computations={%region_4.4_spmd, %region_5.7_spmd} | conditional | flops 276369408 | bytes 12062794 | solution.py:57
  104.4 1.4 fusion
  106.5 2.0 convolution_add_fusion
  109.1 1.2 and_reduce_fusion.2
  111.1 5.0 %conditional.2 = ((f32[8,256,128]{2,1,0:T(8,128)S(1)}, f32[8,256]{1,0:T(8,128)S(1)}, f32[8,256]{1,0:T(8,128)S(1)})) conditional(s32[]{:T(128)} %convert_element_type.36, (f32[8,256,128]{2,1,0:T(8,128)S(1)}, f32[8,256]{1,0:T(8,128)S(1)}, f32[8,256]{1,0:T(8,128)S(1)}) %tuple.65, (pred[8,4,64,256]{3,2,1,0:T(32,128)(4,1)S(1)}, s32[256]{0:T(256)S(1)}, ...), branch_computations={%region_4.4_spmd, %region_5.7_spmd} | conditional | flops 276369408 | bytes 12062794 | solution.py:57
  111.9 1.4 fusion
  114.0 2.0 convolution_add_fusion
  116.6 1.2 and_reduce_fusion.2
  118.6 5.0 %conditional.2 = ((f32[8,256,128]{2,1,0:T(8,128)S(1)}, f32[8,256]{1,0:T(8,128)S(1)}, f32[8,256]{1,0:T(8,128)S(1)})) conditional(s32[]{:T(128)} %convert_element_type.36, (f32[8,256,128]{2,1,0:T(8,128)S(1)}, f32[8,256]{1,0:T(8,128)S(1)}, f32[8,256]{1,0:T(8,128)S(1)}) %tuple.65, (pred[8,4,64,256]{3,2,1,0:T(32,128)(4,1)S(1)}, s32[256]{0:T(256)S(1)}, ...), branch_computations={%region_4.4_spmd, %region_5.7_spmd} | conditional | flops 276369408 | bytes 12062794 | solution.py:57
  119.5 1.4 fusion
  121.6 2.0 convolution_add_fusion
  124.2 1.2 and_reduce_fusion.2
  126.1 5.0 %conditional.2 = ((f32[8,256,128]{2,1,0:T(8,128)S(1)}, f32[8,256]{1,0:T(8,128)S(1)}, f32[8,256]{1,0:T(8,128)S(1)})) conditional(s32[]{:T(128)} %convert_element_type.36, (f32[8,256,128]{2,1,0:T(8,128)S(1)}, f32[8,256]{1,0:T(8,128)S(1)}, f32[8,256]{1,0:T(8,128)S(1)}) %tuple.65, (pred[8,4,64,256]{3,2,1,0:T(32,128)(4,1)S(1)}, s32[256]{0:T(256)S(1)}, ...), branch_computations={%region_4.4_spmd, %region_5.7_spmd} | conditional | flops 276369408 | bytes 12062794 | solution.py:57
  127.0 1.4 fusion
  129.1 2.0 convolution_add_fusion
  131.7 1.2 and_reduce_fusion.2
  133.7 5.0 %conditional.2 = ((f32[8,256,128]{2,1,0:T(8,128)S(1)}, f32[8,256]{1,0:T(8,128)S(1)}, f32[8,256]{1,0:T(8,128)S(1)})) conditional(s32[]{:T(128)} %convert_element_type.36, (f32[8,256,128]{2,1,0:T(8,128)S(1)}, f32[8,256]{1,0:T(8,128)S(1)}, f32[8,256]{1,0:T(8,128)S(1)}) %tuple.65, (pred[8,4,64,256]{3,2,1,0:T(32,128)(4,1)S(1)}, s32[256]{0:T(256)S(1)}, ...), branch_computations={%region_4.4_spmd, %region_5.7_spmd} | conditional | flops 276369408 | bytes 12062794 | solution.py:57
  134.5 1.4 fusion
  136.6 2.0 convolution_add_fusion
  139.2 1.2 and_reduce_fusion.2
  141.2 5.0 %conditional.2 = ((f32[8,256,128]{2,1,0:T(8,128)S(1)}, f32[8,256]{1,0:T(8,128)S(1)}, f32[8,256]{1,0:T(8,128)S(1)})) conditional(s32[]{:T(128)} %convert_element_type.36, (f32[8,256,128]{2,1,0:T(8,128)S(1)}, f32[8,256]{1,0:T(8,128)S(1)}, f32[8,256]{1,0:T(8,128)S(1)}) %tuple.65, (pred[8,4,64,256]{3,2,1,0:T(32,128)(4,1)S(1)}, s32[256]{0:T(256)S(1)}, ...), branch_computations={%region_4.4_spmd, %region_5.7_spmd} | conditional | flops 276369408 | bytes 12062794 | solution.py:57
  142.1 1.4 fusion
  144.2 2.0 convolution_add_fusion
  146.8 1.2 and_reduce_fusion.2
  148.7 5.0 %conditional.2 = ((f32[8,256,128]{2,1,0:T(8,128)S(1)}, f32[8,256]{1,0:T(8,128)S(1)}, f32[8,256]{1,0:T(8,128)S(1)})) conditional(s32[]{:T(128)} %convert_element_type.36, (f32[8,256,128]{2,1,0:T(8,128)S(1)}, f32[8,256]{1,0:T(8,128)S(1)}, f32[8,256]{1,0:T(8,128)S(1)}) %tuple.65, (pred[8,4,64,256]{3,2,1,0:T(32,128)(4,1)S(1)}, s32[256]{0:T(256)S(1)}, ...), branch_computations={%region_4.4_spmd, %region_5.7_spmd} | conditional | flops 276369408 | bytes 12062794 | solution.py:57
  149.6 1.4 fusion
  151.7 2.0 convolution_add_fusion
  154.3 1.2 and_reduce_fusion.2
  156.3 5.0 %conditional.2 = ((f32[8,256,128]{2,1,0:T(8,128)S(1)}, f32[8,256]{1,0:T(8,128)S(1)}, f32[8,256]{1,0:T(8,128)S(1)})) conditional(s32[]{:T(128)} %convert_element_type.36, (f32[8,256,128]{2,1,0:T(8,128)S(1)}, f32[8,256]{1,0:T(8,128)S(1)}, f32[8,256]{1,0:T(8,128)S(1)}) %tuple.65, (pred[8,4,64,256]{3,2,1,0:T(32,128)(4,1)S(1)}, s32[256]{0:T(256)S(1)}, ...), branch_computations={%region_4.4_spmd, %region_5.7_spmd} | conditional | flops 276369408 | bytes 12062794 | solution.py:57
  157.1 1.4 fusion
  159.2 2.0 convolution_add_fusion
  161.9 1.2 and_reduce_fusion.2
  163.8 5.0 %conditional.2 = ((f32[8,256,128]{2,1,0:T(8,128)S(1)}, f32[8,256]{1,0:T(8,128)S(1)}, f32[8,256]{1,0:T(8,128)S(1)})) conditional(s32[]{:T(128)} %convert_element_type.36, (f32[8,256,128]{2,1,0:T(8,128)S(1)}, f32[8,256]{1,0:T(8,128)S(1)}, f32[8,256]{1,0:T(8,128)S(1)}) %tuple.65, (pred[8,4,64,256]{3,2,1,0:T(32,128)(4,1)S(1)}, s32[256]{0:T(256)S(1)}, ...), branch_computations={%region_4.4_spmd, %region_5.7_spmd} | conditional | flops 276369408 | bytes 12062794 | solution.py:57
  164.7 1.4 fusion
  166.8 2.0 convolution_add_fusion
  171.3 5.0 %conditional.2 = ((f32[8,256,128]{2,1,0:T(8,128)S(1)}, f32[8,256]{1,0:T(8,128)S(1)}, f32[8,256]{1,0:T(8,128)S(1)})) conditional(s32[]{:T(128)} %convert_element_type.36, (f32[8,256,128]{2,1,0:T(8,128)S(1)}, f32[8,256]{1,0:T(8,128)S(1)}, f32[8,256]{1,0:T(8,128)S(1)}) %tuple.65, (pred[8,4,64,256]{3,2,1,0:T(32,128)(4,1)S(1)}, s32[256]{0:T(256)S(1)}, ...), branch_computations={%region_4.4_spmd, %region_5.7_spmd} | conditional | flops 276369408 | bytes 12062794 | solution.py:57
  172.2 1.4 fusion
  174.3 2.0 convolution_add_fusion
  178.9 5.0 %conditional.2 = ((f32[8,256,128]{2,1,0:T(8,128)S(1)}, f32[8,256]{1,0:T(8,128)S(1)}, f32[8,256]{1,0:T(8,128)S(1)})) conditional(s32[]{:T(128)} %convert_element_type.36, (f32[8,256,128]{2,1,0:T(8,128)S(1)}, f32[8,256]{1,0:T(8,128)S(1)}, f32[8,256]{1,0:T(8,128)S(1)}) %tuple.65, (pred[8,4,64,256]{3,2,1,0:T(32,128)(4,1)S(1)}, s32[256]{0:T(256)S(1)}, ...), branch_computations={%region_4.4_spmd, %region_5.7_spmd} | conditional | flops 276369408 | bytes 12062794 | solution.py:57
  179.7 1.4 fusion
  181.8 2.0 convolution_add_fusion
  186.4 5.0 %conditional.2 = ((f32[8,256,128]{2,1,0:T(8,128)S(1)}, f32[8,256]{1,0:T(8,128)S(1)}, f32[8,256]{1,0:T(8,128)S(1)})) conditional(s32[]{:T(128)} %convert_element_type.36, (f32[8,256,128]{2,1,0:T(8,128)S(1)}, f32[8,256]{1,0:T(8,128)S(1)}, f32[8,256]{1,0:T(8,128)S(1)}) %tuple.65, (pred[8,4,64,256]{3,2,1,0:T(32,128)(4,1)S(1)}, s32[256]{0:T(256)S(1)}, ...), branch_computations={%region_4.4_spmd, %region_5.7_spmd} | conditional | flops 276369408 | bytes 12062794 | solution.py:57
  187.3 1.4 fusion
  189.4 2.0 convolution_add_fusion
  194.0 5.0 %conditional.2 = ((f32[8,256,128]{2,1,0:T(8,128)S(1)}, f32[8,256]{1,0:T(8,128)S(1)}, f32[8,256]{1,0:T(8,128)S(1)})) conditional(s32[]{:T(128)} %convert_element_type.36, (f32[8,256,128]{2,1,0:T(8,128)S(1)}, f32[8,256]{1,0:T(8,128)S(1)}, f32[8,256]{1,0:T(8,128)S(1)}) %tuple.65, (pred[8,4,64,256]{3,2,1,0:T(32,128)(4,1)S(1)}, s32[256]{0:T(256)S(1)}, ...), branch_computations={%region_4.4_spmd, %region_5.7_spmd} | conditional | flops 276369408 | bytes 12062794 | solution.py:57
  194.8 1.4 fusion
  196.9 2.0 convolution_add_fusion
  199.5 1.2 and_reduce_fusion.2
  201.5 5.0 %conditional.2 = ((f32[8,256,128]{2,1,0:T(8,128)S(1)}, f32[8,256]{1,0:T(8,128)S(1)}, f32[8,256]{1,0:T(8,128)S(1)})) conditional(s32[]{:T(128)} %convert_element_type.36, (f32[8,256,128]{2,1,0:T(8,128)S(1)}, f32[8,256]{1,0:T(8,128)S(1)}, f32[8,256]{1,0:T(8,128)S(1)}) %tuple.65, (pred[8,4,64,256]{3,2,1,0:T(32,128)(4,1)S(1)}, s32[256]{0:T(256)S(1)}, ...), branch_computations={%region_4.4_spmd, %region_5.7_spmd} | conditional | flops 276369408 | bytes 12062794 | solution.py:57
  202.3 1.4 fusion
  204.4 2.0 convolution_add_fusion
  (289 shorter events, 42.3 us)
Async XLA Ops:
  6.5 79.3 %copy-start.1 = (s32[8,8]{1,0:T(8,128)S(1)}, s32[8,8]{1,0:T(8,128)}, u32[]{:S(2)}) copy-start(s32[8,8]{1,0:T(8,128)} %param.13) | copy-start | bytes 772
  6.5 79.3 %copy-start = (s32[8,8]{1,0:T(8,128)S(1)}, s32[8,8]{1,0:T(8,128)}, u32[]{:S(2)}) copy-start(s32[8,8]{1,0:T(8,128)} %param.12) | copy-start | bytes 772
  6.5 40.2 %all-gather.3.cloned.1.call-start = ((), (), s32[]{:S(2)}) async-start(), calls=%async_computation | async-start | bytes 1114112 | tf_op jit(solution)/shard_map/all_gather | solution.py:93
  7.3 78.5 %all-gather.5.cloned.1.call-start = ((), (), s32[]{:S(2)}) async-start(), calls=%async_computation.1 | async-start | bytes 1114112 | tf_op jit(solution)/shard_map/all_gather | solution.py:94
Sparse Core Ops, SparseCore 0:
  9.5 37.2 all-gather.2
  48.9 36.8 all-gather.4
where the time goes:
time: 216 us; the launch traced here: 214 us
  waiting for transfers between devices  77.6 us (36%)
  matrix products  54.5 us (25%)
  other arithmetic  41.2 us (19%)
  local copies, waits for them, and re-layouts  15.1 us (7%)
  between operations  13.5 us (6%)
  loops' own time  12.4 us (6%)
    all_gather x1, waiting for transfers between devices, shards(): lax.all_gather(value_rows, ('outer', 'inner'), axis=0, tiled=True)  39 us
    all_gather x1, waiting for transfers between devices, shards(): lax.all_gather(key_rows, ('outer', 'inner'), axis=0, tiled=True)  37.2 us
    dot_general x16, matrix products, update(): jnp.einsum('hqk,kd->hqd', weights.astype(jnp.bfloat16), value_part, prefe...  31.6 us
    dot_general x16, matrix products, update(): jnp.einsum('qhd,kd->hqk', query_heads, key_part, preferred_element_type=j...  22.9 us
    reduce_or x16, other arithmetic, attend_block(): return lax.cond(jnp.any(allowed), update, keep_same, running)  18.9 us
    and x32, local copies, waits for them, and re-layouts, attend_block(): live_blocks[:, :, None, :] & causal[None]  12.1 us
    another operation x1, loops' own time, attend_piece(): return lax.fori_loop(0, length // sub_rows, one_part, running)  11.2 us
    reduce_sum x16, other arithmetic, update(): new_total = run_total * rescale + jnp.sum(weights, axis=-1)  10.2 us
  transfers between devices with their start and end apart: 2, of which 2 were waited for; matrix products, arithmetic and copies ran while one was open for 1% of the time, Pallas kernels for 0%

commit v1 on v0

v1 whole, which is shorter than its diff:
```python
import functools
import math

import jax
import jax.numpy as jnp
from jax import lax
from jax.experimental import pallas as pl
from jax.experimental.pallas import tpu as pltpu
from jax.sharding import PartitionSpec as P

BLK = 64
DEAD = -1e30
MESH = pl.DeviceIdType.MESH


def relay(sizes, k_hbm, v_hbm, kv, local_sem, zs, zr, ys, yr, cs, cr):
    Z, W, C = sizes
    R = k_hbm.shape[0]
    part = lax.axis_index("parts")
    outer = lax.axis_index("outer")
    c = lax.axis_index("inner")
    z, y = outer // W, outer % W

    def rows(zz, yy, cc):
        return pl.ds(pl.multiple_of(((zz * W + yy) * C + cc) * R, R), R)

    loads = [
        pltpu.make_async_copy(k_hbm, kv.at[0, rows(z, y, c)], local_sem.at[0]),
        pltpu.make_async_copy(v_hbm, kv.at[1, rows(z, y, c)], local_sem.at[1]),
    ]
    for load in loads:
        load.start()

    up = (part, (z + 1) * W + y, c)
    down = (part, (z - 1) * W + y, c)
    across = (part, z * W + (1 - y), c)
    twin = (part, outer, 1 - c)

    barrier = pltpu.get_barrier_semaphore()

    def greet(who):
        pl.semaphore_signal(barrier, inc=1, device_id=who, device_id_type=MESH)

    greet(twin)
    if W == 2:
        greet(across)

    @pl.when(z > 0)
    def _():
        greet(down)

    @pl.when(z < Z - 1)
    def _():
        greet(up)

    pl.semaphore_wait(
        barrier, W + jnp.where(z > 0, 1, 0) + jnp.where(z < Z - 1, 1, 0)
    )

    def copy(t, where, who, send, recv, own=False):
        return pltpu.make_async_remote_copy(
            src_ref=(k_hbm, v_hbm)[t] if own else kv.at[t, where], dst_ref=kv.at[t, where],
            send_sem=send, recv_sem=recv, device_id=who, device_id_type=MESH,
        )

    def z_copy(t, zz, own=False):
        return copy(t, rows(zz, y, c), up, zs.at[t, zz], zr.at[t, zz], own)

    def y_copy(t, zz, yy, own=False):
        return copy(t, rows(zz, yy, c), across, ys.at[t, zz], yr.at[t, zz], own)

    def c_copy(t, zz, yy, cc, own=False):
        return copy(t, rows(zz, yy, cc), twin, cs.at[t, yy, zz], cr.at[t, yy, zz], own)

    def send_shard(t, zz, own):
        @pl.when(z < Z - 1)
        def _():
            z_copy(t, zz, own).start()

        if W == 2:
            if own:
                @pl.when(y == 0)
                def _():
                    y_copy(t, zz, y, True).start()
            else:
                y_copy(t, zz, y).start()
        if own:
            @pl.when(c == 0)
            def _():
                c_copy(t, zz, y, c, True).start()
        else:
            c_copy(t, zz, y, c).start()

    for t in range(2):
        send_shard(t, z, True)

    def relay_across(zz):
        for t in range(2):
            y_copy(t, zz, 1 - y).wait_recv()
            c_copy(t, zz, 1 - y, c).start()

    def step(j, carry):
        zz = z - j
        for t in range(2):
            z_copy(t, zz).wait_recv()
            send_shard(t, zz, False)
        if W == 2:
            @pl.when((j > 1) | (y == 1))
            def _():
                relay_across(zz + 1)
        return carry

    lax.fori_loop(1, z + 1, step, 0)
    if W == 2:
        @pl.when((z > 0) | (y == 1))
        def _():
            relay_across(0)

    def arrivals(zz, carry):
        for t in range(2):
            c_copy(t, zz, y, 1 - c).wait_recv()
            if W == 2:
                c_copy(t, zz, 1 - y, 1 - c).wait_recv()
        return carry

    def sends(zz, carry):
        for t in range(2):
            c_copy(t, zz, y, c).wait_send()
            if W == 2:
                c_copy(t, zz, 1 - y, c).wait_send()
                y_copy(t, zz, y).wait_send()
        return carry

    def z_sends(zz, carry):
        for t in range(2):
            z_copy(t, zz).wait_send()
        return carry

    lax.fori_loop(0, z, arrivals, 0)
    for t in range(2):
        @pl.when(c == 1)
        def _():
            c_copy(t, z, y, 1 - c).wait_recv()

        if W == 2:
            @pl.when(y == 1)
            def _():
                c_copy(t, z, 1 - y, 1 - c).wait_recv()

    for load in loads:
        load.wait()
    lax.fori_loop(0, z, sends, 0)
    for t in range(2):
        @pl.when(c == 0)
        def _():
            c_copy(t, z, y, c).wait_send()

        if W == 2:
            @pl.when(y == 1)
            def _():
                c_copy(t, z, 1 - y, c).wait_send()

            @pl.when(y == 0)
            def _():
                y_copy(t, z, y).wait_send()

    @pl.when(z < Z - 1)
    def _():
        lax.fori_loop(0, z + 1, z_sends, 0)


def attend(vert, slash, q_ref, kv, out, kb_tab, bias_tab):
    heads, nv = vert.shape
    ns = slash.shape[1]
    R = q_ref.shape[0]
    hd = kv.shape[2]
    QB = R // BLK
    NB = kv.shape[1] // BLK
    own_block = (lax.axis_index("outer") * lax.axis_size("inner") + lax.axis_index("inner")) * QB

    def tables(h, carry):
        def compact(ref, n, end):
            vals = [ref[h, s] for s in range(n)]
            drop = [(v == end[0]) | (v == end[1]) for v in vals]
            first = jnp.where(drop[n - 2], vals[n - 1], vals[n - 2])
            res, used = [], None
            for s in range(n - 2):
                if used is None:
                    fill = first
                    used = drop[s]
                else:
                    fill = jnp.where(used, vals[n - 1], first)
                    used = used | drop[s]
                res.append(jnp.where(drop[s], fill, vals[s]))
            return res

        offsets = compact(slash, ns, (0, NB - 1))
        columns = [jnp.int32(0)] + compact(vert, nv, (0, NB - 1))
        for b in range(QB):
            i = own_block + b
            slot = 0
            for o in offsets:
                kb = i - o
                dead = kb < 0
                for col in columns:
                    dead = dead | (kb == col)
                kb_tab[h, b * 16 + slot] = jnp.where(dead, 0, kb)
                bias_tab[h, b * 16 + slot] = jnp.where(dead, DEAD, 0.0).astype(jnp.float32)
                slot += 1
            for col in columns:
                dead = col >= i
                kb_tab[h, b * 16 + slot] = jnp.where(dead, 0, col)
                bias_tab[h, b * 16 + slot] = jnp.where(dead, DEAD, 0.0).astype(jnp.float32)
                slot += 1
        return carry

    lax.fori_loop(0, heads, tables, 0)

    factor = math.log2(math.e) / math.sqrt(hd)
    lane = lax.broadcasted_iota(jnp.int32, (BLK, 2 * BLK), 1)
    row = lax.broadcasted_iota(jnp.int32, (BLK, 2 * BLK), 0)
    left = lane < BLK
    above = left & (lane > row)

    def one_head(h, carry):
        cols = pl.ds(pl.multiple_of(h * hd, hd), hd)
        for b in range(QB):
            q = q_ref[b * BLK:(b + 1) * BLK, cols]
            slots = ns - 2 + nv - 1
            kbs = [own_block + b] + [kb_tab[h, b * 16 + s] for s in range(slots)]
            bias = [None] + [bias_tab[h, b * 16 + s] for s in range(slots)]
            starts = [pl.multiple_of(kb * BLK, BLK) for kb in kbs]
            keys = jnp.concatenate([kv[0, pl.ds(s, BLK), :] for s in starts], axis=0)
            values = jnp.concatenate([kv[1, pl.ds(s, BLK), :] for s in starts], axis=0)
            scores = lax.dot_general(
                q, keys, (((1,), (1,)), ((), ())), preferred_element_type=jnp.float32
            )
            tiles = []
            for g in range(len(kbs) // 2):
                if g == 0:
                    shift = jnp.where(above, DEAD, jnp.where(left, 0.0, bias[1]))
                else:
                    shift = jnp.where(left, bias[2 * g], bias[2 * g + 1])
                tiles.append(scores[:, g * 2 * BLK:(g + 1) * 2 * BLK] * factor + shift)
            top = functools.reduce(jnp.maximum, tiles)
            top = jnp.max(top, axis=1, keepdims=True)
            weights = [jnp.exp2(t - top) for t in tiles]
            total = jnp.sum(functools.reduce(jnp.add, weights), axis=1, keepdims=True)
            rounded = jnp.concatenate([w.astype(jnp.bfloat16) for w in weights], axis=1)
            mixed = jnp.dot(rounded, values, preferred_element_type=jnp.float32)
            out[b * BLK:(b + 1) * BLK, cols] = (mixed * (1.0 / total)).astype(out.dtype)
        return carry

    lax.fori_loop(0, heads, one_head, 0)


def shards(sizes, queries, key_rows, value_rows, vertical, slash_offsets):
    Z, W, C = sizes
    R, hd = key_rows.shape
    heads = vertical.shape[0]
    dma = pltpu.SemaphoreType.DMA
    kv = pl.pallas_call(
        functools.partial(relay, sizes),
        out_shape=jax.ShapeDtypeStruct((2, Z * W * C * R, hd), jnp.bfloat16),
        in_specs=[pl.BlockSpec(memory_space=pltpu.HBM)] * 2,
        out_specs=pl.BlockSpec(memory_space=pl.ANY),
        scratch_shapes=[
            dma((2,)),
            dma((2, Z)), dma((2, Z)),
            dma((2, Z)), dma((2, Z)),
            dma((2, W, Z)), dma((2, W, Z)),
        ],
        compiler_params=pltpu.CompilerParams(
            collective_id=0, has_side_effects=True, vmem_limit_bytes=1 << 20
        ),
    )(key_rows, value_rows)
    smem = pl.BlockSpec(memory_space=pltpu.SMEM)
    vmem = pl.BlockSpec(memory_space=pltpu.VMEM)
    return pl.pallas_call(
        attend,
        out_shape=jax.ShapeDtypeStruct(queries.shape, jnp.bfloat16),
        in_specs=[smem, smem, vmem, vmem],
        out_specs=vmem,
        scratch_shapes=[
            pltpu.SMEM((heads, 16 * (R // BLK)), jnp.int32),
            pltpu.SMEM((heads, 16 * (R // BLK)), jnp.float32),
        ],
        compiler_params=pltpu.CompilerParams(vmem_limit_bytes=32 << 20),
    )(vertical, slash_offsets, queries, kv)


def solution(mesh):
    outer = mesh.shape["outer"]
    columns = 2 if len(mesh.devices) <= 2 and outer % 2 == 0 else 1
    sizes = (outer // columns, columns, mesh.shape["inner"])
    rows = P(("parts", "outer", "inner"), None)
    in_specs = (rows, rows, rows, P("parts", None), P("parts", None))
    return jax.shard_map(
        functools.partial(shards, sizes), mesh=mesh, in_specs=in_specs, out_specs=rows,
        check_vma=False,
    )
```

time: 216 us -> 33.9 us (0.16)
  the two profiles are of different devices: /device:TPU:29 before, /device:TPU:25 now
where the time goes in v1:
time: 33.9 us; the launch traced here: 33.7 us
  Pallas kernels  32 us (94%)
  local copies, waits for them, and re-layouts  1.69 us (5%)
    pallas_call x1, Pallas kernels, shards(): pl.pallas_call(functools.partial(relay, sizes), out_shape=jax.ShapeDtypeS...  17.2 us
    pallas_call x1, Pallas kernels, shards(): pl.pallas_call(attend, out_shape=jax.ShapeDtypeStruct(queries.shape, jnp....  14.8 us
    unnamed x10, local copies, waits for them, and re-layouts  1.69 us

profile of v1, /device:TPU:25, one launch (start us, length us, event | category | flops | bytes accessed | tf_op | source)
XLA Modules:
  0.0 33.7 jit_solution(16633852485296508007)
XLA Ops:
  0.0 0.0 copy-start.1
  0.0 0.8 %copy-done.1 = bf16[256,128]{1,0:T(8,128)(2,1)S(1)} copy-done((bf16[256,128]{1,0:T(8,128)(2,1)S(1)}, bf16[256,128]{1,0:T(8,128)(2,1)}, u32[]{:S(2)}) %copy-start.1) | copy-done | bytes 65560
  0.8 0.0 copy-start.2
  0.8 0.8 %copy-done.2 = bf16[256,128]{1,0:T(8,128)(2,1)S(1)} copy-done((bf16[256,128]{1,0:T(8,128)(2,1)S(1)}, bf16[256,128]{1,0:T(8,128)(2,1)}, u32[]{:S(2)}) %copy-start.2) | copy-done | bytes 65560
  1.7 0.0 copy-start
  1.7 0.0 copy-start.3
  1.7 0.0 copy-start.4
  1.7 17.2 %shard_map.55.kv = bf16[2,4096,128]{2,1,0:T(8,128)(2,1)S(1)} custom-call(bf16[256,128]{1,0:T(8,128)(2,1)S(1)} %copy-done.1, bf16[256,128]{1,0:T(8,128)(2,1)S(1)} %copy-done.2), custom_call_target="tpu_custom_call" | custom-call | tf_op jit(solution)/shard_map/pallas_call | solution.py:262
  18.9 0.0 copy-done
  18.9 0.0 copy-done.3
  18.9 0.0 copy-done.4
  18.9 14.8 %shard_map.56 = bf16[256,1024]{1,0:T(8,128)(2,1)} custom-call(s32[8,8]{1,0:T(8,128)S(1)} %copy-done.3, s32[8,8]{1,0:T(8,128)S(1)} %copy-done.4, bf16[256,1024]{1,0:T(8,128)(2,1)S(1)} %copy-done, bf16[2,4096,128]{2,1,0:T(8,128)(2,1)S(1)} %shard_map.55.kv), custom_call_target="tpu_custom_call" | custom-call | tf_op jit(solution)/shard_map/pallas_call | solution.py:279
Async XLA Ops:
  0.0 0.8 %copy-start.1 = (bf16[256,128]{1,0:T(8,128)(2,1)S(1)}, bf16[256,128]{1,0:T(8,128)(2,1)}, u32[]{:S(2)}) copy-start(bf16[256,128]{1,0:T(8,128)(2,1)} %k_hbm.1) | copy-start | bytes 196612
  0.8 0.8 %copy-start.2 = (bf16[256,128]{1,0:T(8,128)(2,1)S(1)}, bf16[256,128]{1,0:T(8,128)(2,1)}, u32[]{:S(2)}) copy-start(bf16[256,128]{1,0:T(8,128)(2,1)} %v_hbm.1) | copy-start | bytes 196612
  1.7 17.2 %copy-start = (bf16[256,1024]{1,0:T(8,128)(2,1)S(1)}, bf16[256,1024]{1,0:T(8,128)(2,1)}, u32[]{:S(2)}) copy-start(bf16[256,1024]{1,0:T(8,128)(2,1)} %q_ref.1) | copy-start | bytes 1572868
  1.7 17.2 %copy-start.3 = (s32[8,8]{1,0:T(8,128)S(1)}, s32[8,8]{1,0:T(8,128)}, u32[]{:S(2)}) copy-start(s32[8,8]{1,0:T(8,128)} %vert.1) | copy-start | bytes 772
  1.7 17.2 %copy-start.4 = (s32[8,8]{1,0:T(8,128)S(1)}, s32[8,8]{1,0:T(8,128)}, u32[]{:S(2)}) copy-start(s32[8,8]{1,0:T(8,128)} %slash.1) | copy-start | bytes 772

commit v2 on v1

--- a/solution.py
+++ b/solution.py
@@ -10,6 +10,7 @@
 
 BLK = 64
 DEAD = -1e30
+UNROLL = 4
 MESH = pl.DeviceIdType.MESH
 
 
@@ -169,7 +170,7 @@
         lax.fori_loop(0, z + 1, z_sends, 0)
 
 
-def attend(vert, slash, q_ref, kv, out, kb_tab, bias_tab):
+def attend(vert, slash, q_ref, kv, out, marks):
     heads, nv = vert.shape
     ns = slash.shape[1]
     R = q_ref.shape[0]
@@ -178,87 +179,104 @@
     NB = kv.shape[1] // BLK
     own_block = (lax.axis_index("outer") * lax.axis_size("inner") + lax.axis_index("inner")) * QB
 
-    def tables(h, carry):
-        def compact(ref, n, end):
-            vals = [ref[h, s] for s in range(n)]
-            drop = [(v == end[0]) | (v == end[1]) for v in vals]
-            first = jnp.where(drop[n - 2], vals[n - 1], vals[n - 2])
-            res, used = [], None
-            for s in range(n - 2):
-                if used is None:
-                    fill = first
-                    used = drop[s]
-                else:
-                    fill = jnp.where(used, vals[n - 1], first)
-                    used = used | drop[s]
-                res.append(jnp.where(drop[s], fill, vals[s]))
-            return res
-
-        offsets = compact(slash, ns, (0, NB - 1))
-        columns = [jnp.int32(0)] + compact(vert, nv, (0, NB - 1))
-        for b in range(QB):
-            i = own_block + b
-            slot = 0
-            for o in offsets:
-                kb = i - o
-                dead = kb < 0
-                for col in columns:
-                    dead = dead | (kb == col)
-                kb_tab[h, b * 16 + slot] = jnp.where(dead, 0, kb)
-                bias_tab[h, b * 16 + slot] = jnp.where(dead, DEAD, 0.0).astype(jnp.float32)
-                slot += 1
-            for col in columns:
-                dead = col >= i
-                kb_tab[h, b * 16 + slot] = jnp.where(dead, 0, col)
-                bias_tab[h, b * 16 + slot] = jnp.where(dead, DEAD, 0.0).astype(jnp.float32)
-                slot += 1
-        return carry
-
-    lax.fori_loop(0, heads, tables, 0)
+    def clear(n, carry):
+        for u in range(8):
+            marks[n * 8 + u] = -1
+        return carry
+
+    lax.fori_loop(0, NB // 8, clear, 0)
 
     factor = math.log2(math.e) / math.sqrt(hd)
     lane = lax.broadcasted_iota(jnp.int32, (BLK, 2 * BLK), 1)
     row = lax.broadcasted_iota(jnp.int32, (BLK, 2 * BLK), 0)
     left = lane < BLK
     above = left & (lane > row)
-
-    def one_head(h, carry):
+    nt = (((1,), (1,)), ((), ()))
+
+    def compact(ref, h, n):
+        vals = [ref[h, s] for s in range(n)]
+        drop = [(v == 0) | (v == NB - 1) for v in vals]
+        fill = jnp.where(drop[n - 2], vals[n - 1], vals[n - 2])
+        kept = []
+        for s in range(n - 2):
+            kept.append(jnp.where(drop[s], fill, vals[s]))
+            fill = jnp.where(drop[s], vals[n - 1], fill)
+        return kept
+
+    def gather(t, blocks):
+        return jnp.concatenate(
+            [kv[t, pl.ds(pl.multiple_of(kb * BLK, BLK), BLK), :] for kb in blocks], axis=0
+        )
+
+    def dead_bias(dead):
+        return jnp.where(dead, DEAD, 0.0).astype(jnp.float32)
+
+    def one_head(h):
         cols = pl.ds(pl.multiple_of(h * hd, hd), hd)
+        columns = compact(vert, h, nv)
+        offsets = compact(slash, h, ns)
+        for col in columns:
+            marks[col] = h
+        shared = [jnp.minimum(col, own_block + QB - 1) for col in columns]
+        shared_scores = lax.dot_general(
+            q_ref[:, cols], gather(0, shared), nt, preferred_element_type=jnp.float32
+        )
+        shared_values = gather(1, shared)
+        groups = len(columns) // 2
+        shared_weights, own = [], []
         for b in range(QB):
-            q = q_ref[b * BLK:(b + 1) * BLK, cols]
-            slots = ns - 2 + nv - 1
-            kbs = [own_block + b] + [kb_tab[h, b * 16 + s] for s in range(slots)]
-            bias = [None] + [bias_tab[h, b * 16 + s] for s in range(slots)]
-            starts = [pl.multiple_of(kb * BLK, BLK) for kb in kbs]
-            keys = jnp.concatenate([kv[0, pl.ds(s, BLK), :] for s in starts], axis=0)
-            values = jnp.concatenate([kv[1, pl.ds(s, BLK), :] for s in starts], axis=0)
+            i = own_block + b
+            at = slice(b * BLK, (b + 1) * BLK)
+            kbs, bias = [i, jnp.int32(0)], [None, dead_bias(i == 0)]
+            for o in offsets:
+                kb = jnp.maximum(i - o, 0)
+                kbs.append(kb)
+                bias.append(dead_bias((i <= o) | (marks[kb] == h)))
             scores = lax.dot_general(
-                q, keys, (((1,), (1,)), ((), ())), preferred_element_type=jnp.float32
+                q_ref[at, cols], gather(0, kbs), nt, preferred_element_type=jnp.float32
             )
             tiles = []
+            for g in range(groups):
+                d0, d1 = dead_bias(columns[2 * g] >= i), dead_bias(columns[2 * g + 1] >= i)
+                shift = jnp.where(left, d0, d1)
+                tiles.append(shared_scores[at, g * 2 * BLK:(g + 1) * 2 * BLK] * factor + shift)
             for g in range(len(kbs) // 2):
                 if g == 0:
                     shift = jnp.where(above, DEAD, jnp.where(left, 0.0, bias[1]))
                 else:
                     shift = jnp.where(left, bias[2 * g], bias[2 * g + 1])
                 tiles.append(scores[:, g * 2 * BLK:(g + 1) * 2 * BLK] * factor + shift)
-            top = functools.reduce(jnp.maximum, tiles)
-            top = jnp.max(top, axis=1, keepdims=True)
+            top = jnp.max(functools.reduce(jnp.maximum, tiles), axis=1, keepdims=True)
             weights = [jnp.exp2(t - top) for t in tiles]
             total = jnp.sum(functools.reduce(jnp.add, weights), axis=1, keepdims=True)
-            rounded = jnp.concatenate([w.astype(jnp.bfloat16) for w in weights], axis=1)
-            mixed = jnp.dot(rounded, values, preferred_element_type=jnp.float32)
-            out[b * BLK:(b + 1) * BLK, cols] = (mixed * (1.0 / total)).astype(out.dtype)
-        return carry
-
-    lax.fori_loop(0, heads, one_head, 0)
+            rounded = [w.astype(jnp.bfloat16) for w in weights]
+            shared_weights.append(jnp.concatenate(rounded[:groups], axis=1))
+            mixed = jnp.dot(
+                jnp.concatenate(rounded[groups:], axis=1), gather(1, kbs),
+                preferred_element_type=jnp.float32,
+            )
+            own.append((at, mixed, total))
+        shared_mixed = jnp.dot(
+            jnp.concatenate(shared_weights, axis=0), shared_values,
+            preferred_element_type=jnp.float32,
+        )
+        for at, mixed, total in own:
+            out[at, cols] = ((mixed + shared_mixed[at, :]) * (1.0 / total)).astype(out.dtype)
+
+    def some_heads(n, carry):
+        for u in range(UNROLL):
+            one_head(n * UNROLL + u)
+        return carry
+
+    lax.fori_loop(0, heads // UNROLL, some_heads, 0)
 
 
 def shards(sizes, queries, key_rows, value_rows, vertical, slash_offsets):
     Z, W, C = sizes
     R, hd = key_rows.shape
-    heads = vertical.shape[0]
     dma = pltpu.SemaphoreType.DMA
+    key_rows = pltpu.with_memory_space_constraint(key_rows, pltpu.HBM)
+    value_rows = pltpu.with_memory_space_constraint(value_rows, pltpu.HBM)
     kv = pl.pallas_call(
         functools.partial(relay, sizes),
         out_shape=jax.ShapeDtypeStruct((2, Z * W * C * R, hd), jnp.bfloat16),
@@ -282,8 +300,7 @@
         in_specs=[smem, smem, vmem, vmem],
         out_specs=vmem,
         scratch_shapes=[
-            pltpu.SMEM((heads, 16 * (R // BLK)), jnp.int32),
-            pltpu.SMEM((heads, 16 * (R // BLK)), jnp.float32),
+            pltpu.SMEM((Z * W * C * R // BLK,), jnp.int32),
         ],
         compiler_params=pltpu.CompilerParams(vmem_limit_bytes=32 << 20),
     )(vertical, slash_offsets, queries, kv)

time: 33.9 us -> 23.8 us (0.70)
  Pallas kernels: 32 us -> 23.6 us
  local copies, waits for them, and re-layouts: 1.69 us -> 0.01 us
    pallas_call x1, Pallas kernels: 14.8 us -> 6.32 us  [shards(): pl.pallas_call(attend, out_shape=jax.ShapeDtypeStruct(queries.shape, jnp....]
    unnamed x10 -> x6, local copies, waits for them, and re-layouts: 1.69 us -> 0.01 us
where the time goes in v2:
time: 23.8 us; the launch traced here: 23.6 us
  Pallas kernels  23.6 us (99%)
    pallas_call x1, Pallas kernels, shards(): pl.pallas_call(functools.partial(relay, sizes), out_shape=jax.ShapeDtypeS...  17.2 us
    pallas_call x1, Pallas kernels, shards(): pl.pallas_call(attend, out_shape=jax.ShapeDtypeStruct(queries.shape, jnp....  6.32 us

profile of v2, /device:TPU:25, one launch (start us, length us, event | category | flops | bytes accessed | tf_op | source)
XLA Modules:
  0.0 23.6 jit_solution(2721188035047034431)
XLA Ops:
  0.0 0.0 copy-start.2
  0.0 0.0 copy-start.1
  0.0 0.0 copy-start
  0.0 17.2 %shard_map.55.kv = bf16[2,4096,128]{2,1,0:T(8,128)(2,1)S(1)} custom-call(bf16[256,128]{1,0:T(8,128)(2,1)} %k_hbm.1, bf16[256,128]{1,0:T(8,128)(2,1)} %v_hbm.1), custom_call_target="tpu_custom_call" | custom-call | tf_op jit(solution)/shard_map/pallas_call | solution.py:280
  17.3 0.0 copy-done.2
  17.3 0.0 copy-done.1
  17.3 0.0 copy-done
  17.3 6.3 %shard_map.56 = bf16[256,1024]{1,0:T(8,128)(2,1)} custom-call(s32[8,8]{1,0:T(8,128)S(1)} %copy-done.1, s32[8,8]{1,0:T(8,128)S(1)} %copy-done.2, bf16[256,1024]{1,0:T(8,128)(2,1)S(1)} %copy-done, bf16[2,4096,128]{2,1,0:T(8,128)(2,1)S(1)} %shard_map.55.kv), custom_call_target="tpu_custom_call" | custom-call | tf_op jit(solution)/shard_map/pallas_call | solution.py:297
Async XLA Ops:
  0.0 17.3 %copy-start.2 = (s32[8,8]{1,0:T(8,128)S(1)}, s32[8,8]{1,0:T(8,128)}, u32[]{:S(2)}) copy-start(s32[8,8]{1,0:T(8,128)} %slash.1) | copy-start | bytes 772
  0.0 17.3 %copy-start.1 = (s32[8,8]{1,0:T(8,128)S(1)}, s32[8,8]{1,0:T(8,128)}, u32[]{:S(2)}) copy-start(s32[8,8]{1,0:T(8,128)} %vert.1) | copy-start | bytes 772
  0.0 17.3 %copy-start = (bf16[256,1024]{1,0:T(8,128)(2,1)S(1)}, bf16[256,1024]{1,0:T(8,128)(2,1)}, u32[]{:S(2)}) copy-start(bf16[256,1024]{1,0:T(8,128)(2,1)} %q_ref.1) | copy-start | bytes 1572868
